TPU v7x, 256 devices: a whole 4x4x8 slice. The times are simulated.
256 devices in a mesh: expert: 8 (over y, core), dp: 32 (over x, z).
Axes of the slice: x: 4, y: 4, z: 8, core: 2. Of those that a mesh axis runs over, the one named last changes fastest.
Arguments:
- hidden: bfloat16 [8, 14336, 1024], P('expert', 'dp'), may hold values from -6 to 6
- weight_codes: int32 [8, 14336, 2048], P('expert', 'dp'), may hold values from -8 to 7
- group_scales: float32 [8, 448, 2048], P('expert', 'dp'), may hold values from 0.0006681531 to 0.0050111483
- expert_index: int32 [4096, 2], P('expert'), may hold values from 0 to 7, all different within a row
- gate_values: float32 [4096, 2], P('expert'), may hold values from 0.2 to 1
- output_grad: bfloat16 [4096, 2048], P('expert', 'dp'), may hold values from -6 to 6
Outputs:
- combined: bfloat16 [4096, 2048], P('expert', 'dp')
- gate_grad: float32 [4096, 2], P('expert')
- hidden_grad: bfloat16 [8, 14336, 1024], P('expert', 'dp')
- weight_grad: float32 [8, 14336, 2048], P('expert', 'dp')
- scale_grad: float32 [8, 448, 2048], P('expert', 'dp')
Inputs may be any that keep to these rules, and one draw needn't show every extreme that they name: `expert_index`: the 2 entries of a token name different experts.
All inputs are finite; a program needn't handle non-finite values.
Results may differ from a plain program's by a relative error of at most 0.0058.
Values may be sent and summed in bfloat16 or wider, within the bound.
No kernel may reach another device: no remote copies, remote signals or barrier semaphores. Data moves between devices by JAX's collectives and lax.ppermute only.
A program may use at most 128 MiB of HBM per device.

v0:
```python
import jax
import jax.numpy as jnp
from jax import lax
from jax.sharding import PartitionSpec as P

EXPERTS = 8
GROUP = 32


def dequantize(weight_codes, group_scales):
    experts_here, units_here, feature_width = weight_codes.shape
    grouped = weight_codes.astype(jnp.float32).reshape(
        experts_here, units_here // GROUP, GROUP, feature_width
    )
    return (
        (grouped * group_scales[:, :, None, :])
        .reshape(experts_here, units_here, feature_width)
        .astype(jnp.bfloat16)
    )


def choice_ranks(flat_experts):
    onehot = (flat_experts[:, None] == jnp.arange(EXPERTS, dtype=jnp.int32)[None, :]).astype(
        jnp.int32
    )
    return jnp.sum((jnp.cumsum(onehot, axis=0) - onehot) * onehot, axis=1)


def on_device(hidden, weight_codes, group_scales, expert_index, gate_values, output_grad):
    local_experts = hidden.shape[0]
    slot_total = hidden.shape[2]
    feature_width = weight_codes.shape[2]
    expert_groups = lax.axis_size("expert")
    data_ranks = lax.axis_size("dp")
    tokens_here, choices = expert_index.shape
    capacity = tokens_here * choices // EXPERTS
    column_count = feature_width // data_ranks
    weight_table = dequantize(weight_codes, group_scales)
    table_cols = weight_table
    partial_value = jnp.einsum(
        "efs,efd->des", hidden, table_cols, preferred_element_type=jnp.float32
    )
    summed = lax.psum(partial_value.reshape(feature_width, local_experts * slot_total), "dp")
    owned_rows = lax.dynamic_slice_in_dim(
        summed, lax.axis_index("dp") * column_count, column_count, 0
    )
    outgoing = owned_rows.astype(jnp.bfloat16).reshape(column_count, local_experts, slot_total)
    returned = lax.all_to_all(outgoing, "expert", split_axis=2, concat_axis=2, tiled=True)
    returned = returned.reshape(column_count, local_experts * slot_total)
    flat_experts = expert_index.reshape(-1)
    ranking = choice_ranks(flat_experts)
    kept_mask = ranking < capacity
    clipped = jnp.minimum(ranking, capacity - 1)
    group_of = flat_experts // local_experts
    within = flat_experts % local_experts
    columns = jnp.arange(EXPERTS * capacity, dtype=jnp.int32)
    place_index = (within * expert_groups + group_of) * capacity + clipped
    picker = ((place_index[:, None] == columns[None, :]) & kept_mask[:, None]).astype(jnp.bfloat16)
    gathered = jnp.einsum("ac,dc->ad", picker, returned, preferred_element_type=jnp.float32)
    gathered = gathered.reshape(tokens_here, choices, column_count)
    keep_float = kept_mask.reshape(tokens_here, choices).astype(jnp.float32)
    weighted = gate_values * keep_float
    grad_float = output_grad.astype(jnp.float32)
    combined = jnp.sum(weighted[:, :, None] * gathered, axis=1).astype(jnp.bfloat16)
    gate_partial = keep_float * jnp.sum(grad_float[:, None, :] * gathered, axis=2)
    gate_grad = lax.psum(gate_partial, "dp")
    values = (
        (weighted[:, :, None] * grad_float[:, None, :])
        .reshape(tokens_here * choices, column_count)
        .astype(jnp.bfloat16)
    )
    outbound = jnp.einsum("ac,ad->cd", picker, values, preferred_element_type=jnp.float32).astype(
        jnp.bfloat16
    )
    outbound = outbound.reshape(local_experts, slot_total, column_count)
    arrived = lax.all_to_all(outbound, "expert", split_axis=1, concat_axis=1, tiled=True)
    block_cols = lax.all_gather(arrived, "dp", axis=2, tiled=True)
    table_cols = weight_table
    hidden_acc = jnp.einsum(
        "esd,efd->efs", block_cols, table_cols, preferred_element_type=jnp.float32
    )
    weight_piece = jnp.einsum(
        "efs,esd->efd", hidden, block_cols, preferred_element_type=jnp.float32
    )
    hidden_acc, weight_grad = (hidden_acc, weight_piece)
    hidden_grad = hidden_acc.astype(jnp.bfloat16)
    products = weight_grad * weight_codes.astype(jnp.float32)
    scale_grad = jnp.sum(products.reshape(local_experts, -1, GROUP, feature_width), axis=2)
    return (combined, gate_grad, hidden_grad, weight_grad, scale_grad)


def solution(mesh):
    return jax.shard_map(
        on_device,
        mesh=mesh,
        in_specs=(
            P("expert", "dp", None),
            P("expert", "dp", None),
            P("expert", "dp", None),
            P("expert", None),
            P("expert", None),
            P("expert", "dp"),
        ),
        out_specs=(
            P("expert", "dp"),
            P("expert", None),
            P("expert", "dp", None),
            P("expert", "dp", None),
            P("expert", "dp", None),
        ),
        check_vma=False,
    )
```

profile of v0, /device:TPU:8, one launch (start us, length us, event | category | flops | bytes accessed | tf_op | source)
XLA Modules:
  0.0 422.4 jit_solution(741626494181359657)
XLA Ops:
  7.2 0.9 copy.63
  8.5 2.3 reduce-window.6
  10.8 0.3 slice_reduce_fusion
  11.7 0.7 broadcast_select_fusion.1
  12.8 1.0 copy.77
  14.0 1.2 fusion.29
  15.2 0.4 copy.73
  15.6 0.5 broadcast.133
  16.1 2.3 reduce.3
  18.6 9.4 %all_to_all.10 = bf16[8,2,4096]{2,1,0:T(2,128)(2,1)S(1)} all-to-all(bf16[8,2,4096]{2,1,0:T(2,128)(2,1)S(1)} %reshape.142), channel_id=1, replica_groups=mesh['expert'=8,'dp'=32] {'expert'}, dimensions={0} | all-to-all | bytes 262144 | tf_op jit(solution)/shard_map/all_to_all | solution.py:76
  28.0 0.3 reshape.143
  28.4 0.9 copy.74
  29.3 0.6 convert_element_type.45
  30.4 82.7 %all-gather.2.cloned.1.call-done = bf16[1,1024,2048]{1,2,0:T(8,128)(2,1)} async-done(((bf16[1,1024,64]{1,2,0:T(8,128)(2,1)}), bf16[1,1024,2048]{1,2,0:T(8,128)(2,1)}) %all-gather.2.cloned.1.call-update) | async-done | bytes 4194320 | tf_op jit(solution)/shard_map/all_gather | solution.py:77
  113.1 4.3 %fusion.12 = f32[1,448,2048]{2,1,0:T(8,128)S(1)} fusion(bf16[1,1024,2048]{1,2,0:T(8,128)(2,1)} %all-gather.2.cloned.1.call-done, bf16[1,448,1024]{2,1,0:T(8,128)(2,1)S(1)} %copy-done), kind=kOutput, calls=%fused_computation.14 | convolution fusion | flops 1879048192 | bytes 8781824 | tf_op jit(solution)/shard_map/efs,esd->efd/dot_general | solution.py:82
  117.4 0.4 mul.82
  117.8 2.9 copy-done.1
  120.7 3.1 convert_multiply_fusion
  123.9 5.6 %fusion.33 = f32[2048,1024]{1,0:T(8,128)} fusion(bf16[448,2048]{1,0:T(8,128)(2,1)S(1)} %get-tuple-element.13, bf16[1,448,1024]{2,1,0:T(8,128)(2,1)S(1)} %copy-done), kind=kOutput, calls=%fused_computation.25 | convolution fusion | flops 1879048192 | bytes 11141120 | tf_op jit(solution)/shard_map/efs,efd->des/dot_general | solution.py:40
  129.5 192.6 %all-reduce.1 = bf16[2048,1024]{1,0:T(8,128)(2,1)} all-reduce(f32[2048,1024]{1,0:T(8,128)} %fusion.33), channel_id=1, replica_groups=mesh['expert'=8,'dp'=32] {'dp'}, use_global_device_ids=true, to_apply=%region_3.4 | all-reduce | flops 2097152 | bytes 12582912 | tf_op jit(solution)/shard_map/psum | solution.py:43
  322.1 0.9 fusion.36
  323.0 0.4 copy.68
  323.4 2.4 reduce.4
  325.8 0.9 reshape.140
  326.7 4.8 %all-to-all-start = ((bf16[8,2,4096]{2,1,0:T(2,128)(2,1)}), bf16[8,2,4096]{2,1,0:T(2,128)(2,1)S(1)}, u32[]{:S(2)}, u32[]{:S(2)}) async-start(bf16[8,2,4096]{2,1,0:T(2,128)(2,1)} %reshape.140), calls=%async_computation | async-start | bytes 262144 | tf_op jit(solution)/shard_map/all_to_all | solution.py:48
  331.5 5.2 %fusion.23 = bf16[1,448,1024]{2,1,0:T(8,128)(2,1)} fusion(bf16[448,2048]{1,0:T(8,128)(2,1)S(1)} %get-tuple-element.13, bf16[1,1024,2048]{1,2,0:T(8,128)(2,1)} %all-gather.2.cloned.1.call-done), kind=kOutput, calls=%fused_computation.21 | convolution fusion | flops 1879506944 | bytes 6946816 | tf_op jit(solution)/shard_map/esd,efd->efs/dot_general | solution.py:79
  336.7 2.6 reduce_sum.41
  339.3 0.7 reduce_sum.42
  340.0 0.3 reshape.141
  340.3 0.3 copy.69
  340.7 2.0 multiply_reduce_fusion
  342.7 72.9 %psum.15 = f32[512,2]{0,1:T(2,128)} all-reduce(f32[512,2]{0,1:T(2,128)S(1)} %broadcast_select_fusion), channel_id=1, replica_groups=mesh['expert'=8,'dp'=32] {'dp'}, use_global_device_ids=true, to_apply=%region_6.7 | all-reduce | flops 1024 | bytes 8192 | tf_op jit(solution)/shard_map/psum | solution.py:66
  (35 shorter events, 2.2 us)
Async XLA Ops:
  7.2 105.9 %copy-start = (bf16[1,448,1024]{2,1,0:T(8,128)(2,1)S(1)}, bf16[1,448,1024]{2,1,0:T(8,128)(2,1)}, u32[]{:S(2)}) copy-start(bf16[1,448,1024]{2,1,0:T(8,128)(2,1)} %param.6) | copy-start | bytes 2752516
  7.2 105.9 %all-gather.2.cloned.1.call-start = ((), (), s32[]{:S(2)}) async-start(), calls=%async_computation.2 | async-start | bytes 4325376 | tf_op jit(solution)/shard_map/all_gather | solution.py:77
  12.8 16.6 %copy-start.3 = (bf16[512,64]{0,1:T(8,128)(2,1)S(1)}, bf16[512,64]{0,1:T(8,128)(2,1)}, u32[]{:S(2)}) copy-start(bf16[512,64]{0,1:T(8,128)(2,1)} %param.11) | copy-start | bytes 196612
  13.8 16.2 %copy-start.5 = (f32[1,14,2048]{2,0,1:T(1,128)S(1)}, f32[1,14,2048]{2,0,1:T(1,128)}, u32[]{:S(2)}) copy-start(f32[1,14,2048]{2,0,1:T(1,128)} %param.8) | copy-start | bytes 344068
  14.0 16.4 %copy-start.6 = (s32[512,2]{0,1:T(2,128)S(1)}, s32[512,2]{0,1:T(2,128)}, u32[]{:S(2)}) copy-start(s32[512,2]{0,1:T(2,128)} %param.9) | copy-start | bytes 12292
  117.3 6.5 %copy-start.2 = (f32[1,448,2048]{2,1,0:T(8,128)}, f32[1,448,2048]{2,1,0:T(8,128)S(1)}, u32[]{:S(2)}) copy-start(f32[1,448,2048]{2,1,0:T(8,128)S(1)} %fusion.12) | copy-start | bytes 11010052
  117.4 3.4 copy-start.1
  326.7 13.3 %all-to-all-start = ((bf16[8,2,4096]{2,1,0:T(2,128)(2,1)}), bf16[8,2,4096]{2,1,0:T(2,128)(2,1)S(1)}, u32[]{:S(2)}, u32[]{:S(2)}) async-start(bf16[8,2,4096]{2,1,0:T(2,128)(2,1)} %reshape.140), calls=%async_computation | async-start | bytes 262144 | tf_op jit(solution)/shard_map/all_to_all | solution.py:48
  336.7 4.0 copy-start.4
Sparse Core Ops, SparseCore 0:
  29.4 83.5 all-gather.1
where the time goes:
time: 423 us; the launch traced here: 422 us
  blocking collectives  275 us (65%)
  waiting for transfers between devices  82.7 us (20%)
  matrix products  18.3 us (4%)
  other arithmetic  14.3 us (3%)
  between operations  14.3 us (3%)
  local copies, waits for them, and re-layouts  13.1 us (3%)
  starting transfers between devices  4.84 us (1%)
    psum x1, blocking collectives, on_device(): lax.psum(partial_value.reshape(feature_width, local_experts * slot_total)...  193 us
    all_gather x1, waiting for transfers between devices, on_device(): block_cols = lax.all_gather(arrived, 'dp', axis=2, tiled=True)  82.7 us
    psum x1, blocking collectives, on_device(): gate_grad = lax.psum(gate_partial, 'dp')  72.9 us
    all_to_all x1, blocking collectives, on_device(): lax.all_to_all(outbound, 'expert', split_axis=1, concat_axis=1, tiled=True)  9.39 us
  transfers between devices with their start and end apart: 2, of which 1 were waited for; matrix products, arithmetic and copies ran while one was open for 2% of the time, Pallas kernels for 0%

commit v1 on v0

--- a/solution.py
+++ b/solution.py
@@ -73,7 +73,9 @@
         jnp.bfloat16
     )
     outbound = outbound.reshape(local_experts, slot_total, column_count)
-    arrived = lax.all_to_all(outbound, "expert", split_axis=1, concat_axis=1, tiled=True)
+    cells = jnp.split(outbound, lax.axis_size("expert"), axis=1)
+    received = lax.all_to_all(jnp.stack(cells), "expert", 0, 0)
+    arrived = jnp.concatenate(received, axis=1)
     block_cols = lax.all_gather(arrived, "dp", axis=2, tiled=True)
     table_cols = weight_table
     hidden_acc = jnp.einsum(

time: 423 us -> 419 us (level)
  no operation moved by 1% of the time
where the time goes in v1:
time: 419 us
  blocking collectives  275 us (66%)
  waiting for transfers between devices  82.7 us (20%)
  matrix products  18.3 us (4%)
  between operations  14.3 us (3%)
  local copies, waits for them, and re-layouts  11.9 us (3%)
  other arithmetic  11.9 us (3%)
  starting transfers between devices  4.86 us (1%)
    psum x1, blocking collectives, on_device(): lax.psum(partial_value.reshape(feature_width, local_experts * slot_total)...  192 us
    all_gather x1, waiting for transfers between devices, on_device(): block_cols = lax.all_gather(arrived, 'dp', axis=2, tiled=True)  82.7 us
    psum x1, blocking collectives, on_device(): gate_grad = lax.psum(gate_partial, 'dp')  72.9 us
    all_to_all x1, blocking collectives, on_device(): received = lax.all_to_all(jnp.stack(cells), 'expert', 0, 0)  9.39 us
  transfers between devices with their start and end apart: 2, of which 1 were waited for; matrix products, arithmetic and copies ran while one was open for 2% of the time, Pallas kernels for 0%

profile of v1, /device:TPU:8, one launch (start us, length us, event | category | flops | bytes accessed | tf_op | source)
XLA Modules:
  0.0 418.6 jit_solution(11756204937589890643)
XLA Ops:
  7.3 0.9 copy.35
  8.5 2.3 reduce-window.6
  10.8 0.3 slice_reduce_fusion
  11.4 0.3 lt.20
  11.8 0.7 broadcast_select_fusion.1
  12.8 0.9 copy.47
  13.7 0.2 mul.87.clone
  13.9 1.2 fusion.29
  15.3 9.4 %all_to_all.10 = bf16[8,1,128,64]{2,3,1,0:T(8,128)(2,1)S(1)} all-to-all(bf16[8,1,128,64]{2,3,1,0:T(8,128)(2,1)S(1)} %constant_dynamic-update-slice_fusion), channel_id=1, replica_groups=mesh['expert'=8,'dp'=32] {'expert'}, dimensions={0} | all-to-all | bytes 262144 | tf_op jit(solution)/shard_map/all_to_all | solution.py:77
  24.7 0.7 copy_bitcast_fusion
  25.4 0.6 convert_element_type.45
  26.1 0.2 min.16
  26.4 82.7 %all-gather.2.cloned.1.call-done = bf16[1,1024,2048]{1,2,0:T(8,128)(2,1)} async-done(((bf16[1,1024,64]{1,2,0:T(8,128)(2,1)}), bf16[1,1024,2048]{1,2,0:T(8,128)(2,1)}) %all-gather.2.cloned.1.call-update) | async-done | bytes 4194320 | tf_op jit(solution)/shard_map/all_gather | solution.py:79
  109.1 4.3 %fusion.12 = f32[1,448,2048]{2,1,0:T(8,128)S(1)} fusion(bf16[1,1024,2048]{1,2,0:T(8,128)(2,1)} %all-gather.2.cloned.1.call-done, bf16[1,448,1024]{2,1,0:T(8,128)(2,1)S(1)} %copy-done), kind=kOutput, calls=%fused_computation.14 | convolution fusion | flops 1879048192 | bytes 8781824 | tf_op jit(solution)/shard_map/efs,esd->efd/dot_general | solution.py:84
  113.4 0.4 mul.82
  113.9 2.9 copy-done.1
  116.8 3.1 convert_multiply_fusion
  119.9 5.6 %fusion.33 = f32[2048,1024]{1,0:T(8,128)} fusion(bf16[448,2048]{1,0:T(8,128)(2,1)S(1)} %get-tuple-element.13, bf16[1,448,1024]{2,1,0:T(8,128)(2,1)S(1)} %copy-done), kind=kOutput, calls=%fused_computation.25 | convolution fusion | flops 1879048192 | bytes 11141120 | tf_op jit(solution)/shard_map/efs,efd->des/dot_general | solution.py:40
  125.6 192.4 %all-reduce.1 = bf16[2048,1024]{1,0:T(8,128)(2,1)} all-reduce(f32[2048,1024]{1,0:T(8,128)} %fusion.33), channel_id=1, replica_groups=mesh['expert'=8,'dp'=32] {'dp'}, use_global_device_ids=true, to_apply=%region_3.4 | all-reduce | flops 2097152 | bytes 12582912 | tf_op jit(solution)/shard_map/psum | solution.py:43
  318.0 0.9 fusion.36
  318.9 0.4 copy.40
  319.3 0.5 broadcast.133
  319.8 2.3 reduce.3
  322.1 0.9 reshape.144
  323.0 4.8 %all-to-all-start = ((bf16[8,2,4096]{2,1,0:T(2,128)(2,1)}), bf16[8,2,4096]{2,1,0:T(2,128)(2,1)S(1)}, u32[]{:S(2)}, u32[]{:S(2)}) async-start(bf16[8,2,4096]{2,1,0:T(2,128)(2,1)} %reshape.144), calls=%async_computation | async-start | bytes 262144 | tf_op jit(solution)/shard_map/all_to_all | solution.py:48
  327.8 5.2 %fusion.23 = bf16[1,448,1024]{2,1,0:T(8,128)(2,1)} fusion(bf16[448,2048]{1,0:T(8,128)(2,1)S(1)} %get-tuple-element.13, bf16[1,1024,2048]{1,2,0:T(8,128)(2,1)} %all-gather.2.cloned.1.call-done), kind=kOutput, calls=%fused_computation.21 | convolution fusion | flops 1879506944 | bytes 6946816 | tf_op jit(solution)/shard_map/esd,efd->efs/dot_general | solution.py:81
  333.0 2.6 reduce_sum.41
  335.5 0.7 reduce_sum.42
  336.2 0.3 reshape.145
  336.6 0.3 copy.41
  336.9 2.0 multiply_reduce_fusion
  338.9 72.9 %psum.15 = f32[512,2]{0,1:T(2,128)} all-reduce(f32[512,2]{0,1:T(2,128)S(1)} %broadcast_select_fusion), channel_id=1, replica_groups=mesh['expert'=8,'dp'=32] {'dp'}, use_global_device_ids=true, to_apply=%region_6.7 | all-reduce | flops 1024 | bytes 8192 | tf_op jit(solution)/shard_map/psum | solution.py:66
  (39 shorter events, 1.4 us)
Async XLA Ops:
  7.2 102.0 %copy-start = (bf16[1,448,1024]{2,1,0:T(8,128)(2,1)S(1)}, bf16[1,448,1024]{2,1,0:T(8,128)(2,1)}, u32[]{:S(2)}) copy-start(bf16[1,448,1024]{2,1,0:T(8,128)(2,1)} %param.6) | copy-start | bytes 2752516
  7.2 19.2 %copy-start.6 = (s32[512,2]{0,1:T(2,128)S(1)}, s32[512,2]{0,1:T(2,128)}, u32[]{:S(2)}) copy-start(s32[512,2]{0,1:T(2,128)} %param.9) | copy-start | bytes 12292
  7.2 18.2 %copy-start.3 = (bf16[512,64]{0,1:T(8,128)(2,1)S(1)}, bf16[512,64]{0,1:T(8,128)(2,1)}, u32[]{:S(2)}) copy-start(bf16[512,64]{0,1:T(8,128)(2,1)} %param.11) | copy-start | bytes 196612
  7.2 18.8 %copy-start.5 = (f32[1,14,2048]{2,0,1:T(1,128)S(1)}, f32[1,14,2048]{2,0,1:T(1,128)}, u32[]{:S(2)}) copy-start(f32[1,14,2048]{2,0,1:T(1,128)} %param.8) | copy-start | bytes 344068
  7.2 101.9 %all-gather.2.cloned.1.call-start = ((), (), s32[]{:S(2)}) async-start(), calls=%async_computation.2 | async-start | bytes 4325376 | tf_op jit(solution)/shard_map/all_gather | solution.py:79
  113.4 6.5 %copy-start.2 = (f32[1,448,2048]{2,1,0:T(8,128)}, f32[1,448,2048]{2,1,0:T(8,128)S(1)}, u32[]{:S(2)}) copy-start(f32[1,448,2048]{2,1,0:T(8,128)S(1)} %fusion.12) | copy-start | bytes 11010052
  113.4 3.4 copy-start.1
  323.0 13.3 %all-to-all-start = ((bf16[8,2,4096]{2,1,0:T(2,128)(2,1)}), bf16[8,2,4096]{2,1,0:T(2,128)(2,1)S(1)}, u32[]{:S(2)}, u32[]{:S(2)}) async-start(bf16[8,2,4096]{2,1,0:T(2,128)(2,1)} %reshape.144), calls=%async_computation | async-start | bytes 262144 | tf_op jit(solution)/shard_map/all_to_all | solution.py:48
  332.9 3.9 copy-start.4
Sparse Core Ops, SparseCore 0:
  25.5 83.5 all-gather.1

commit v2 on v0

--- a/solution.py
+++ b/solution.py
@@ -5,6 +5,13 @@
 
 EXPERTS = 8
 GROUP = 32
+
+
+def gather_over(x, name, along):
+    peers = lax.axis_size(name)
+    blocks = jnp.stack([x for _ in range(peers)])
+    blocks = lax.all_to_all(blocks, name, split_axis=0, concat_axis=0)
+    return jnp.concatenate(blocks, axis=along)
 
 
 def dequantize(weight_codes, group_scales):
@@ -74,7 +81,7 @@
     )
     outbound = outbound.reshape(local_experts, slot_total, column_count)
     arrived = lax.all_to_all(outbound, "expert", split_axis=1, concat_axis=1, tiled=True)
-    block_cols = lax.all_gather(arrived, "dp", axis=2, tiled=True)
+    block_cols = gather_over(arrived, "dp", 2)
     table_cols = weight_table
     hidden_acc = jnp.einsum(
         "esd,efd->efs", block_cols, table_cols, preferred_element_type=jnp.float32

time: 423 us -> 436 us (1.031)
  between operations: 14.3 us -> 0.87 us
  waiting for transfers between devices: 82.7 us -> 95.7 us
  starting transfers between devices: 4.84 us -> 16.3 us
    all_to_all x0 -> x1, waiting for transfers between devices: none -> 95.7 us  [gather_over(): blocks = lax.all_to_all(blocks, name, split_axis=0, concat_axis=0)]
    all_gather x1 -> x0, waiting for transfers between devices: 82.7 us -> none  [on_device(): block_cols = lax.all_gather(arrived, 'dp', axis=2, tiled=True)]
    all_to_all x0 -> x1, starting transfers between devices: none -> 11.6 us  [gather_over(): blocks = lax.all_to_all(blocks, name, split_axis=0, concat_axis=0)]
where the time goes in v2:
time: 436 us; the launch traced here: 435 us
  blocking collectives  275 us (63%)
  waiting for transfers between devices  95.7 us (22%)
  matrix products  18.3 us (4%)
  starting transfers between devices  16.3 us (4%)
  local copies, waits for them, and re-layouts  14.8 us (3%)
  other arithmetic  14.2 us (3%)
    psum x1, blocking collectives, on_device(): lax.psum(partial_value.reshape(feature_width, local_experts * slot_total)...  192 us
    all_to_all x1, waiting for transfers between devices, gather_over(): blocks = lax.all_to_all(blocks, name, split_axis=0, concat_axis=0)  95.7 us
    psum x1, blocking collectives, on_device(): gate_grad = lax.psum(gate_partial, 'dp')  73.5 us
    all_to_all x1, starting transfers between devices, gather_over(): blocks = lax.all_to_all(blocks, name, split_axis=0, concat_axis=0)  11.6 us
    all_to_all x1, blocking collectives, on_device(): lax.all_to_all(outbound, 'expert', split_axis=1, concat_axis=1, tiled=True)  9.39 us
  transfers between devices with their start and end apart: 2, of which 1 were waited for; matrix products, arithmetic and copies ran while one was open for 2% of the time, Pallas kernels for 0%

profile of v2, /device:TPU:8, one launch (start us, length us, event | category | flops | bytes accessed | tf_op | source)
XLA Modules:
  0.0 435.2 jit_solution(16430309691421586035)
XLA Ops:
  0.6 0.9 copy.52
  1.9 2.3 reduce-window.6
  5.2 0.7 broadcast_select_fusion.1
  6.2 0.9 copy.66
  7.3 1.2 fusion.17
  8.5 0.4 copy.62
  8.9 0.5 broadcast.136
  9.4 2.3 reduce.3
  12.0 9.4 %all_to_all.18 = bf16[8,2,4096]{2,1,0:T(2,128)(2,1)S(1)} all-to-all(bf16[8,2,4096]{2,1,0:T(2,128)(2,1)S(1)} %reshape.152), channel_id=1, replica_groups=mesh['expert'=8,'dp'=32] {'expert'}, dimensions={0} | all-to-all | bytes 262144 | tf_op jit(solution)/shard_map/all_to_all | solution.py:83
  21.7 0.3 copy.63
  22.0 2.5 stack.2
  24.5 11.6 %all-to-all-start.2 = ((bf16[32,1,1024,64]{2,3,1,0:T(8,128)(2,1)}), bf16[32,1,1024,64]{2,3,1,0:T(8,128)(2,1)}, u32[]{:S(2)}, u32[]{:S(2)}) async-start(bf16[32,1,1024,64]{2,3,1,0:T(8,128)(2,1)} %stack.2), calls=%async_computation.2 | async-start | bytes 8388608 | tf_op jit(solution)/shard_map/all_to_all | solution.py:13
  36.1 0.6 convert_element_type.45
  37.1 95.7 %all-to-all-done.2 = bf16[32,1,1024,64]{2,3,1,0:T(8,128)(2,1)} async-done(((bf16[32,1,1024,64]{2,3,1,0:T(8,128)(2,1)}), bf16[32,1,1024,64]{2,3,1,0:T(8,128)(2,1)}, u32[]{:S(2)}, u32[]{:S(2)}) %all-to-all-start.2) | async-done | bytes 4194336 | tf_op jit(solution)/shard_map/all_to_all | solution.py:13
  132.8 4.3 convolution_bitcast_fusion
  137.1 0.4 mul.82
  137.6 2.9 copy-done.1
  140.5 3.1 convert_multiply_fusion
  143.6 5.6 %fusion.21 = f32[2048,1024]{1,0:T(8,128)} fusion(bf16[448,2048]{1,0:T(8,128)(2,1)S(1)} %get-tuple-element.13, bf16[1,448,1024]{2,1,0:T(8,128)(2,1)S(1)} %copy-done), kind=kOutput, calls=%fused_computation.21 | convolution fusion | flops 1879048192 | bytes 11141120 | tf_op jit(solution)/shard_map/efs,efd->des/dot_general | solution.py:47
  149.2 192.1 %all-reduce.1 = bf16[2048,1024]{1,0:T(8,128)(2,1)} all-reduce(f32[2048,1024]{1,0:T(8,128)} %fusion.21), channel_id=1, replica_groups=mesh['expert'=8,'dp'=32] {'dp'}, use_global_device_ids=true, to_apply=%region_3.4 | all-reduce | flops 2097152 | bytes 12582912 | tf_op jit(solution)/shard_map/psum | solution.py:50
  341.3 0.9 fusion.24
  342.2 0.4 copy.57
  342.6 2.3 reduce.4
  344.9 0.9 reshape.150
  345.8 4.8 %all-to-all-start = ((bf16[8,2,4096]{2,1,0:T(2,128)(2,1)}), bf16[8,2,4096]{2,1,0:T(2,128)(2,1)S(1)}, u32[]{:S(2)}, u32[]{:S(2)}) async-start(bf16[8,2,4096]{2,1,0:T(2,128)(2,1)} %reshape.150), calls=%async_computation | async-start | bytes 262144 | tf_op jit(solution)/shard_map/all_to_all | solution.py:55
  350.6 5.2 %fusion.13 = bf16[1,448,1024]{2,1,0:T(8,128)(2,1)} fusion(bf16[448,2048]{1,0:T(8,128)(2,1)S(1)} %get-tuple-element.13, bf16[1024,2048]{0,1:T(8,128)(2,1)} %bitcast.13), kind=kOutput, calls=%fused_computation.17 | convolution fusion | flops 1879506944 | bytes 6946816 | tf_op jit(solution)/shard_map/esd,efd->efs/dot_general | solution.py:86
  355.7 2.6 reduce_sum.41
  358.3 0.7 reduce_sum.42
  359.0 0.3 reshape.151
  359.3 0.3 copy.58
  359.7 2.0 multiply_reduce_fusion
  361.7 73.5 %psum.15 = f32[512,2]{0,1:T(2,128)} all-reduce(f32[512,2]{0,1:T(2,128)S(1)} %broadcast_select_fusion), channel_id=1, replica_groups=mesh['expert'=8,'dp'=32] {'dp'}, use_global_device_ids=true, to_apply=%region_6.7 | all-reduce | flops 1024 | bytes 8192 | tf_op jit(solution)/shard_map/psum | solution.py:73
  (35 shorter events, 2.7 us)
Async XLA Ops:
  0.6 132.2 %copy-start = (bf16[1,448,1024]{2,1,0:T(8,128)(2,1)S(1)}, bf16[1,448,1024]{2,1,0:T(8,128)(2,1)}, u32[]{:S(2)}) copy-start(bf16[1,448,1024]{2,1,0:T(8,128)(2,1)} %param.6) | copy-start | bytes 2752516
  24.5 11.6 %copy-start.3 = (bf16[512,64]{0,1:T(8,128)(2,1)S(1)}, bf16[512,64]{0,1:T(8,128)(2,1)}, u32[]{:S(2)}) copy-start(bf16[512,64]{0,1:T(8,128)(2,1)} %param.11) | copy-start | bytes 196612
  24.5 12.2 %copy-start.5 = (f32[1,14,2048]{2,0,1:T(1,128)S(1)}, f32[1,14,2048]{2,0,1:T(1,128)}, u32[]{:S(2)}) copy-start(f32[1,14,2048]{2,0,1:T(1,128)} %param.8) | copy-start | bytes 344068
  24.5 12.6 %copy-start.6 = (s32[512,2]{0,1:T(2,128)S(1)}, s32[512,2]{0,1:T(2,128)}, u32[]{:S(2)}) copy-start(s32[512,2]{0,1:T(2,128)} %param.9) | copy-start | bytes 12292
  24.5 108.3 %all-to-all-start.2 = ((bf16[32,1,1024,64]{2,3,1,0:T(8,128)(2,1)}), bf16[32,1,1024,64]{2,3,1,0:T(8,128)(2,1)}, u32[]{:S(2)}, u32[]{:S(2)}) async-start(bf16[32,1,1024,64]{2,3,1,0:T(8,128)(2,1)} %stack.2), calls=%async_computation.2 | async-start | bytes 8388608 | tf_op jit(solution)/shard_map/all_to_all | solution.py:13
  137.1 6.5 %copy-start.2 = (f32[1,448,2048]{2,1,0:T(8,128)}, f32[1,448,2048]{2,1,0:T(8,128)S(1)}, u32[]{:S(2)}) copy-start(f32[1,448,2048]{2,1,0:T(8,128)S(1)} %convolution_bitcast_fusion) | copy-start | bytes 11010052
  137.1 3.4 copy-start.1
  345.8 13.2 %all-to-all-start = ((bf16[8,2,4096]{2,1,0:T(2,128)(2,1)}), bf16[8,2,4096]{2,1,0:T(2,128)(2,1)S(1)}, u32[]{:S(2)}, u32[]{:S(2)}) async-start(bf16[8,2,4096]{2,1,0:T(2,128)(2,1)} %reshape.150), calls=%async_computation | async-start | bytes 262144 | tf_op jit(solution)/shard_map/all_to_all | solution.py:55
  355.7 3.9 copy-start.4
